TPU v7x, 128 devices: a whole 4x4x4 slice. The times are simulated.
128 devices in a mesh: row: 8 (over z, x_hi), col: 16 (over y, x_lo, core).
Axes of the slice: x: 4 (x_hi: 2, x_lo: 2; x = x_hi * 2 + x_lo), y: 4, z: 4, core: 2. Of those that a mesh axis runs over, the one named last changes fastest.
Arguments:
- features: bfloat16 [32768, 512], P('row'), may hold values from -6 to 6
- logits: float32 [32768, 128], P(('row', 'col')), may hold values from -16 to 16
Outputs:
- memberships: float32 [32768, 128], P(('row', 'col'))
- standardized: float32 [32768, 128], P(('row', 'col'))
All inputs are finite; a program needn't handle non-finite values.
Results may differ from a plain program's by a relative error of at most 0.0003.
Values may be sent and summed in bfloat16 or wider, within the bound.
A program may use at most 64 MiB of HBM per device.

v0:
```python
import math
import jax
import jax.numpy as jnp
from jax import lax
from jax.sharding import PartitionSpec as P

ITERS = 2


def kernel_product(left_rows, right_rows, members):
    count = left_rows.shape[0]
    feature_width = left_rows.shape[1]
    block_rows = math.gcd(count, 512)
    blocks = left_rows.reshape(count // block_rows, block_rows, feature_width)

    def block_product(block):
        inner = jnp.einsum("bf,nf->bn", block, right_rows, preferred_element_type=jnp.float32)
        base = 1.0 + inner / feature_width
        kernel = base * base * base
        return jnp.dot(
            kernel, members, precision=lax.Precision.HIGHEST, preferred_element_type=jnp.float32
        )

    return lax.map(block_product, blocks).reshape(count, members.shape[1])


def on_device(features, logits):
    frames = logits.shape[0]
    column = lax.axis_index("col")
    own_rows = lax.dynamic_slice_in_dim(features, column * frames, frames, 0)
    column_panel = lax.all_gather(own_rows, "row", axis=0, tiled=True)
    raised = jnp.exp(logits)
    members = raised / jnp.sum(raised, axis=1, keepdims=True)
    standardized = members
    for iteration in range(ITERS):
        members_column = lax.all_gather(members, "row", axis=0, tiled=True)
        scores = lax.psum_scatter(
            kernel_product(features, column_panel, members_column),
            "col",
            scatter_dimension=0,
            tiled=True,
        )
        cluster_size, weighted = lax.psum(
            (jnp.sum(members, axis=0), jnp.sum(members * scores, axis=0)), ("row", "col")
        )
        compact = weighted / (cluster_size * cluster_size)
        distance = compact[None, :] - 2.0 * scores / cluster_size[None, :]
        centered = distance - jnp.mean(distance, axis=1, keepdims=True)
        spread = jnp.mean(centered * centered, axis=1, keepdims=True)
        standardized = centered / jnp.sqrt(spread + 1e-06)
        raised = jnp.exp(-2.0 * standardized)
        members = raised / jnp.sum(raised, axis=1, keepdims=True)
    return (members, standardized)


def solution(mesh):
    return jax.shard_map(
        on_device,
        mesh=mesh,
        in_specs=(P("row", None), P(("row", "col"), None)),
        out_specs=(P(("row", "col"), None), P(("row", "col"), None)),
        check_vma=False,
    )
```

profile of v0, /device:TPU:1, one launch (start us, length us, event | category | flops | bytes accessed | tf_op | source)
XLA Modules:
  0.0 545.2 jit_solution(2299477837792060629)
XLA Ops:
  7.2 0.0 all-gather.6.cloned.1.call-start
  7.2 1.0 exponential_reduce_fusion
  8.2 1.7 exponential_divide_fusion
  9.9 0.0 all-gather.6.cloned.1.call-update
  9.9 0.0 all-gather.4.cloned.1.call-start
  10.0 1.7 constant_dynamic-slice_fusion
  11.7 0.0 reduce-scatter.3.cloned.1.call-start
  11.7 47.2 %all-gather.6.cloned.1.call-done = f32[2048,128]{1,0:T(8,128)} async-done(((f32[256,128]{1,0:T(8,128)}), f32[2048,128]{1,0:T(8,128)}) %all-gather.6.cloned.1.call-update) | async-done | bytes 1048592 | tf_op jit(solution)/shard_map/all_gather | solution.py:36
  59.0 55.7 %all-gather.4.cloned.1.call-done = bf16[2048,512]{1,0:T(8,128)(2,1)} async-done(((bf16[256,512]{1,0:T(8,128)(2,1)}), bf16[2048,512]{1,0:T(8,128)(2,1)}) %all-gather.4.cloned.1.call-update) | async-done | bytes 2097168 | tf_op jit(solution)/shard_map/all_gather | solution.py:31
  114.7 0.1 broadcast.70.clone
  114.8 54.8 %while.20 = (s32[]{:T(128)}, f32[8,512,128]{2,1,0:T(8,128)S(1)}, bf16[8,512,512]{2,1,0:T(8,128)(2,1)}, bf16[2048,512]{1,0:T(8,128)(2,1)}, f32[2048,128]{1,0:T(8,128)}, /*index=5*/s32[]{:T(128)}) while((s32[]{:T(128)}, f32[8,512,128]{2,1,0:T(8,128)S(1)}, bf16[8,512,512]{2,1,0:T(8,128)(2,1)}, bf16[2048,512]{1,0:T(8,128)(2,1)}, ...), condition=%wide.region_2.3_spmd, body=%wide.region_1.2_spmd.sunk | while | flops 2688548864 | bytes 16515685 | solution.py:24
  114.9 3.1 fusion.48
  118.0 3.7 fusion.49
  121.7 3.1 fusion.48
  124.9 3.7 fusion.49
  128.6 3.1 fusion.48
  131.7 3.7 fusion.49
  135.4 3.1 fusion.48
  138.6 3.7 fusion.49
  142.3 3.1 fusion.48
  145.4 3.7 fusion.49
  149.1 3.1 fusion.48
  152.3 3.7 fusion.49
  156.0 3.1 fusion.48
  159.1 3.7 fusion.49
  162.8 3.1 fusion.48
  166.0 3.7 fusion.49
  169.7 1.3 copy-done.1
  171.0 0.0 all-gather.8.cloned.1.call-start
  171.0 60.5 %reduce-scatter.3.cloned.1.call-done = f32[256,128]{1,0:T(8,128)} async-done(((f32[4096,128]{1,0:T(8,128)}), f32[256,128]{1,0:T(8,128)}) %reduce-scatter.3.cloned.1.call-update) | async-done | bytes 131088 | tf_op jit(solution)/shard_map/reduce_scatter | solution.py:37
  231.5 1.0 multiply_reduce_fusion.3
  232.5 68.0 %all-reduce.1 = (f32[128]{0:T(128)S(1)}, f32[128]{0:T(128)S(1)}) all-reduce(f32[128]{0:T(128)S(1)} %get-tuple-element.61, f32[128]{0:T(128)S(1)} %get-tuple-element.60), channel_id=1, replica_groups=mesh['row'=8,'col'=16] {'row','col'}, use_global_device_ids=true, to_apply=%region_7.8 | all-reduce | flops 256 | bytes 2048 | tf_op jit(solution)/shard_map/psum | solution.py:43
  300.6 1.0 fusion.30
  301.6 1.1 multiply_reduce_fusion.2
  302.7 1.1 fusion.28
  303.8 1.7 broadcast_divide_fusion
  305.6 0.2 reduce-scatter.5.cloned.1.call-start
  305.8 41.2 %all-gather.8.cloned.1.call-done = f32[2048,128]{1,0:T(8,128)} async-done(((f32[256,128]{1,0:T(8,128)}), f32[2048,128]{1,0:T(8,128)}) %all-gather.8.cloned.1.call-update) | async-done | bytes 1048592 | tf_op jit(solution)/shard_map/all_gather | solution.py:36
  347.0 0.1 broadcast.70
  347.2 54.8 %while.21 = (s32[]{:T(128)}, f32[8,512,128]{2,1,0:T(8,128)S(1)}, bf16[8,512,512]{2,1,0:T(8,128)(2,1)}, bf16[2048,512]{1,0:T(8,128)(2,1)}, f32[2048,128]{1,0:T(8,128)}, /*index=5*/s32[]{:T(128)}) while((s32[]{:T(128)}, f32[8,512,128]{2,1,0:T(8,128)S(1)}, bf16[8,512,512]{2,1,0:T(8,128)(2,1)}, bf16[2048,512]{1,0:T(8,128)(2,1)}, ...), condition=%wide.region_12.13_spmd, body=%wide.region_11.12_spmd.sunk | while | flops 2688548864 | bytes 16515685 | solution.py:24
  347.2 3.1 fusion.53
  350.3 3.7 fusion.54
  354.1 3.1 fusion.53
  357.2 3.7 fusion.54
  360.9 3.1 fusion.53
  364.1 3.7 fusion.54
  367.8 3.1 fusion.53
  370.9 3.7 fusion.54
  374.6 3.1 fusion.53
  377.8 3.7 fusion.54
  381.5 3.1 fusion.53
  384.6 3.7 fusion.54
  388.3 3.1 fusion.53
  391.5 3.7 fusion.54
  395.2 3.1 fusion.53
  398.3 3.7 fusion.54
  402.0 1.3 copy-done
  403.4 62.6 %reduce-scatter.5.cloned.1.call-done = f32[256,128]{1,0:T(8,128)} async-done(((f32[4096,128]{1,0:T(8,128)}), f32[256,128]{1,0:T(8,128)}) %reduce-scatter.5.cloned.1.call-update) | async-done | bytes 131088 | tf_op jit(solution)/shard_map/reduce_scatter | solution.py:37
  466.0 1.1 multiply_reduce_fusion.1
  467.1 67.5 %all-reduce = (f32[128]{0:T(128)S(1)}, f32[128]{0:T(128)S(1)}) all-reduce(f32[128]{0:T(128)S(1)} %get-tuple-element.59, f32[128]{0:T(128)S(1)} %get-tuple-element.58), channel_id=1, replica_groups=mesh['row'=8,'col'=16] {'row','col'}, use_global_device_ids=true, to_apply=%region_17.18 | all-reduce | flops 256 | bytes 2048 | tf_op jit(solution)/shard_map/psum | solution.py:43
  534.6 1.0 fusion.29
  535.6 1.1 multiply_reduce_fusion
  536.7 1.1 fusion.27
  537.9 0.8 fusion.26
  (50 shorter events, 0.2 us)
Async XLA Ops:
  7.2 51.8 %all-gather.6.cloned.1.call-start = ((), (), s32[]{:S(2)}) async-start(), calls=%async_computation.3 | async-start | bytes 1179648 | tf_op jit(solution)/shard_map/all_gather | solution.py:36
  9.9 104.8 %all-gather.4.cloned.1.call-start = ((), (), s32[]{:S(2)}) async-start(), calls=%async_computation.2 | async-start | bytes 2359296 | tf_op jit(solution)/shard_map/all_gather | solution.py:31
  11.7 219.8 %reduce-scatter.3.cloned.1.call-start = ((), (), s32[]{:S(2)}) async-start(), calls=%async_computation.4 | async-start | bytes 2228224 | tf_op jit(solution)/shard_map/reduce_scatter | solution.py:37
  114.8 116.7 %copy-start.3 = (f32[256,128]{1,0:T(8,128)S(1)}, f32[256,128]{1,0:T(8,128)}, u32[]{:S(2)}) copy-start(f32[256,128]{1,0:T(8,128)} %param.7) | copy-start | bytes 393220
  114.8 3.1 copy-start.5
  121.7 3.1 copy-start.5
  128.6 3.1 copy-start.5
  135.4 3.1 copy-start.5
  142.3 3.1 copy-start.5
  149.1 3.1 copy-start.5
  156.0 3.1 copy-start.5
  162.8 3.1 copy-start.5
  169.7 1.3 copy-start.1
  171.0 176.0 %all-gather.8.cloned.1.call-start = ((), (), s32[]{:S(2)}) async-start(), calls=%async_computation.5 | async-start | bytes 1179648 | tf_op jit(solution)/shard_map/all_gather | solution.py:36
  305.6 160.4 %reduce-scatter.5.cloned.1.call-start = ((), (), s32[]{:S(2)}) async-start(), calls=%async_computation.6 | async-start | bytes 2228224 | tf_op jit(solution)/shard_map/reduce_scatter | solution.py:37
  347.2 118.8 %copy-start.2 = (f32[256,128]{1,0:T(8,128)S(1)}, f32[256,128]{1,0:T(8,128)}, u32[]{:S(2)}) copy-start(f32[256,128]{1,0:T(8,128)} %reduce-scatter.3.cloned.1.call-done) | copy-start | bytes 393220
  347.2 3.1 copy-start.6
  354.1 3.1 copy-start.6
  360.9 3.1 copy-start.6
  367.8 3.1 copy-start.6
  374.6 3.1 copy-start.6
  381.5 3.1 copy-start.6
  388.3 3.1 copy-start.6
  395.2 3.1 copy-start.6
  402.0 1.4 copy-start
  537.9 0.8 copy-start.4
Sparse Core Ops, SparseCore 0:
  10.9 48.0 all-gather.5
  61.3 53.3 all-gather.3
  171.1 60.3 reduce-scatter.2
  305.7 41.2 all-gather.7
  403.5 62.4 reduce-scatter.4
where the time goes:
time: 546 us; the launch traced here: 545 us
  waiting for transfers between devices  267 us (49%)
  blocking collectives  136 us (25%)
  matrix products  109 us (20%)
  between operations  13.9 us (3%)
  other arithmetic  13.8 us (3%)
    psum x2, blocking collectives, on_device(): lax.psum((jnp.sum(members, axis=0), jnp.sum(members * scores, axis=0)), (...  136 us
    reduce_scatter x2, waiting for transfers between devices, on_device(): lax.psum_scatter(kernel_product(features, column_panel, members_column),...  123 us
    all_gather x2, waiting for transfers between devices, on_device(): members_column = lax.all_gather(members, 'row', axis=0, tiled=True)  88.4 us
    dot_general x16, matrix products, block_product(): jnp.dot(kernel, members, precision=lax.Precision.HIGHEST, preferred_eleme...  58.9 us
    all_gather x1, waiting for transfers between devices, on_device(): column_panel = lax.all_gather(own_rows, 'row', axis=0, tiled=True)  55.7 us
    dot_general x16, matrix products, block_product(): jnp.einsum('bf,nf->bn', block, right_rows, preferred_element_type=jnp.flo...  50 us
  transfers between devices with their start and end apart: 5, of which 5 were waited for; matrix products, arithmetic and copies ran while one was open for 0% of the time, Pallas kernels for 0%

commit v1 on v0

--- a/solution.py
+++ b/solution.py
@@ -3,6 +3,7 @@
 import jax.numpy as jnp
 from jax import lax
 from jax.sharding import PartitionSpec as P
+from jax.lax import psum
 
 ITERS = 2
 
@@ -40,8 +41,8 @@
             scatter_dimension=0,
             tiled=True,
         )
-        cluster_size, weighted = lax.psum(
-            (jnp.sum(members, axis=0), jnp.sum(members * scores, axis=0)), ("row", "col")
+        cluster_size, weighted = psum(
+            psum((jnp.sum(members, axis=0), jnp.sum(members * scores, axis=0)), "col"), "row"
         )
         compact = weighted / (cluster_size * cluster_size)
         distance = compact[None, :] - 2.0 * scores / cluster_size[None, :]

time: 546 us -> 517 us (0.947)
  blocking collectives: 136 us -> 102 us
    psum x2 -> x4, blocking collectives: 136 us -> 102 us  [the longest x2 60.9 us: on_device(): psum((jnp.sum(members, axis=0), jnp.sum(members * scores, axis=0)), 'col')]
where the time goes in v1:
time: 517 us; the launch traced here: 513 us
  waiting for transfers between devices  269 us (52%)
  matrix products  109 us (21%)
  blocking collectives  102 us (20%)
  between operations  13.9 us (3%)
  other arithmetic  13.8 us (3%)
    reduce_scatter x2, waiting for transfers between devices, on_device(): lax.psum_scatter(kernel_product(features, column_panel, members_column),...  123 us
    all_gather x2, waiting for transfers between devices, on_device(): members_column = lax.all_gather(members, 'row', axis=0, tiled=True)  90.4 us
    psum x2, blocking collectives, on_device(): psum((jnp.sum(members, axis=0), jnp.sum(members * scores, axis=0)), 'col')  60.9 us
    dot_general x16, matrix products, block_product(): jnp.dot(kernel, members, precision=lax.Precision.HIGHEST, preferred_eleme...  58.9 us
    all_gather x1, waiting for transfers between devices, on_device(): column_panel = lax.all_gather(own_rows, 'row', axis=0, tiled=True)  55.7 us
    dot_general x16, matrix products, block_product(): jnp.einsum('bf,nf->bn', block, right_rows, preferred_element_type=jnp.flo...  50 us
    psum x2, blocking collectives, on_device(): psum(psum((jnp.sum(members, axis=0), jnp.sum(members * scores, axis=0)),...  40.8 us
  transfers between devices with their start and end apart: 5, of which 5 were waited for; matrix products, arithmetic and copies ran while one was open for 0% of the time, Pallas kernels for 0%

profile of v1, /device:TPU:1, one launch (start us, length us, event | category | flops | bytes accessed | tf_op | source)
XLA Modules:
  0.0 513.0 jit_solution(9180798623922746307)
XLA Ops:
  7.2 1.0 exponential_reduce_fusion
  8.2 1.7 exponential_divide_fusion
  9.9 0.0 all-gather.4.cloned.1.call-start
  10.0 1.7 constant_dynamic-slice_fusion
  11.7 0.0 reduce-scatter.3.cloned.1.call-start
  11.7 47.2 %all-gather.6.cloned.1.call-done = f32[2048,128]{1,0:T(8,128)} async-done(((f32[256,128]{1,0:T(8,128)}), f32[2048,128]{1,0:T(8,128)}) %all-gather.6.cloned.1.call-update) | async-done | bytes 1048592 | tf_op jit(solution)/shard_map/all_gather | solution.py:37
  59.0 55.7 %all-gather.4.cloned.1.call-done = bf16[2048,512]{1,0:T(8,128)(2,1)} async-done(((bf16[256,512]{1,0:T(8,128)(2,1)}), bf16[2048,512]{1,0:T(8,128)(2,1)}) %all-gather.4.cloned.1.call-update) | async-done | bytes 2097168 | tf_op jit(solution)/shard_map/all_gather | solution.py:32
  114.7 0.1 broadcast.70.clone
  114.8 54.8 %while.20 = (s32[]{:T(128)}, f32[8,512,128]{2,1,0:T(8,128)S(1)}, bf16[8,512,512]{2,1,0:T(8,128)(2,1)}, bf16[2048,512]{1,0:T(8,128)(2,1)}, f32[2048,128]{1,0:T(8,128)}, /*index=5*/s32[]{:T(128)}) while((s32[]{:T(128)}, f32[8,512,128]{2,1,0:T(8,128)S(1)}, bf16[8,512,512]{2,1,0:T(8,128)(2,1)}, bf16[2048,512]{1,0:T(8,128)(2,1)}, ...), condition=%wide.region_2.3_spmd, body=%wide.region_1.2_spmd.sunk | while | flops 2688548864 | bytes 16515685 | solution.py:25
  114.9 3.1 fusion.48
  118.0 3.7 fusion.49
  121.7 3.1 fusion.48
  124.9 3.7 fusion.49
  128.6 3.1 fusion.48
  131.7 3.7 fusion.49
  135.4 3.1 fusion.48
  138.6 3.7 fusion.49
  142.3 3.1 fusion.48
  145.4 3.7 fusion.49
  149.1 3.1 fusion.48
  152.3 3.7 fusion.49
  156.0 3.1 fusion.48
  159.1 3.7 fusion.49
  162.8 3.1 fusion.48
  166.0 3.7 fusion.49
  169.7 1.3 copy-done.1
  171.0 0.0 all-gather.8.cloned.1.call-start
  171.0 60.5 %reduce-scatter.3.cloned.1.call-done = f32[256,128]{1,0:T(8,128)} async-done(((f32[4096,128]{1,0:T(8,128)}), f32[256,128]{1,0:T(8,128)}) %reduce-scatter.3.cloned.1.call-update) | async-done | bytes 131088 | tf_op jit(solution)/shard_map/reduce_scatter | solution.py:38
  231.5 1.0 multiply_reduce_fusion.3
  232.6 30.5 %all-reduce.1 = (f32[128]{0:T(128)S(1)}, f32[128]{0:T(128)S(1)}) all-reduce(f32[128]{0:T(128)S(1)} %get-tuple-element.61, f32[128]{0:T(128)S(1)} %get-tuple-element.60), channel_id=1, replica_groups=mesh['row'=8,'col'=16] {'col'}, use_global_device_ids=true, to_apply=%region_8.9 | all-reduce | flops 256 | bytes 2048 | tf_op jit(solution)/shard_map/psum | solution.py:45
  263.0 20.3 %all-reduce.3 = (f32[128]{0:T(128)S(1)}, f32[128]{0:T(128)S(1)}) all-reduce(f32[128]{0:T(128)S(1)} %get-tuple-element.84, f32[128]{0:T(128)S(1)} %get-tuple-element.85), channel_id=1, replica_groups=mesh['row'=8,'col'=16] {'row'}, use_global_device_ids=true, to_apply=%region_9.10 | all-reduce | flops 256 | bytes 2048 | tf_op jit(solution)/shard_map/psum | solution.py:44
  283.4 1.0 fusion.30
  284.4 1.1 multiply_reduce_fusion.2
  285.5 1.1 fusion.28
  286.7 1.7 broadcast_divide_fusion
  288.4 0.0 reduce-scatter.5.cloned.1.call-start
  288.5 43.2 %all-gather.8.cloned.1.call-done = f32[2048,128]{1,0:T(8,128)} async-done(((f32[256,128]{1,0:T(8,128)}), f32[2048,128]{1,0:T(8,128)}) %all-gather.8.cloned.1.call-update) | async-done | bytes 1048592 | tf_op jit(solution)/shard_map/all_gather | solution.py:37
  331.7 0.1 broadcast.70
  331.8 54.8 %while.21 = (s32[]{:T(128)}, f32[8,512,128]{2,1,0:T(8,128)S(1)}, bf16[8,512,512]{2,1,0:T(8,128)(2,1)}, bf16[2048,512]{1,0:T(8,128)(2,1)}, f32[2048,128]{1,0:T(8,128)}, /*index=5*/s32[]{:T(128)}) while((s32[]{:T(128)}, f32[8,512,128]{2,1,0:T(8,128)S(1)}, bf16[8,512,512]{2,1,0:T(8,128)(2,1)}, bf16[2048,512]{1,0:T(8,128)(2,1)}, ...), condition=%wide.region_14.15_spmd, body=%wide.region_13.14_spmd.sunk | while | flops 2688548864 | bytes 16515685 | solution.py:25
  331.8 3.1 fusion.53
  335.0 3.7 fusion.54
  338.7 3.1 fusion.53
  341.8 3.7 fusion.54
  345.6 3.1 fusion.53
  348.7 3.7 fusion.54
  352.4 3.1 fusion.53
  355.5 3.7 fusion.54
  359.3 3.1 fusion.53
  362.4 3.7 fusion.54
  366.1 3.1 fusion.53
  369.3 3.7 fusion.54
  373.0 3.1 fusion.53
  376.1 3.7 fusion.54
  379.8 3.1 fusion.53
  383.0 3.7 fusion.54
  386.7 1.3 copy-done
  388.0 62.5 %reduce-scatter.5.cloned.1.call-done = f32[256,128]{1,0:T(8,128)} async-done(((f32[4096,128]{1,0:T(8,128)}), f32[256,128]{1,0:T(8,128)}) %reduce-scatter.5.cloned.1.call-update) | async-done | bytes 131088 | tf_op jit(solution)/shard_map/reduce_scatter | solution.py:38
  450.5 1.1 multiply_reduce_fusion.1
  451.6 30.4 %all-reduce = (f32[128]{0:T(128)S(1)}, f32[128]{0:T(128)S(1)}) all-reduce(f32[128]{0:T(128)S(1)} %get-tuple-element.59, f32[128]{0:T(128)S(1)} %get-tuple-element.58), channel_id=1, replica_groups=mesh['row'=8,'col'=16] {'col'}, use_global_device_ids=true, to_apply=%region_20.21 | all-reduce | flops 256 | bytes 2048 | tf_op jit(solution)/shard_map/psum | solution.py:45
  482.0 20.4 %all-reduce.2 = (f32[128]{0:T(128)S(1)}, f32[128]{0:T(128)S(1)}) all-reduce(f32[128]{0:T(128)S(1)} %get-tuple-element.82, f32[128]{0:T(128)S(1)} %get-tuple-element.83), channel_id=1, replica_groups=mesh['row'=8,'col'=16] {'row'}, use_global_device_ids=true, to_apply=%region_21.22 | all-reduce | flops 256 | bytes 2048 | tf_op jit(solution)/shard_map/psum | solution.py:44
  502.4 1.0 fusion.29
  503.5 1.1 multiply_reduce_fusion
  504.6 1.1 fusion.27
  505.7 0.8 fusion.26
  (52 shorter events, 0.3 us)
Async XLA Ops:
  7.2 51.8 %all-gather.6.cloned.1.call-start = ((), (), s32[]{:S(2)}) async-start(), calls=%async_computation.3 | async-start | bytes 1179648 | tf_op jit(solution)/shard_map/all_gather | solution.py:37
  9.9 104.8 %all-gather.4.cloned.1.call-start = ((), (), s32[]{:S(2)}) async-start(), calls=%async_computation.2 | async-start | bytes 2359296 | tf_op jit(solution)/shard_map/all_gather | solution.py:32
  11.7 219.8 %reduce-scatter.3.cloned.1.call-start = ((), (), s32[]{:S(2)}) async-start(), calls=%async_computation.4 | async-start | bytes 2228224 | tf_op jit(solution)/shard_map/reduce_scatter | solution.py:38
  114.8 116.7 %copy-start.3 = (f32[256,128]{1,0:T(8,128)S(1)}, f32[256,128]{1,0:T(8,128)}, u32[]{:S(2)}) copy-start(f32[256,128]{1,0:T(8,128)} %param.7) | copy-start | bytes 393220
  114.8 3.1 copy-start.5
  121.7 3.1 copy-start.5
  128.6 3.1 copy-start.5
  135.4 3.1 copy-start.5
  142.3 3.1 copy-start.5
  149.1 3.1 copy-start.5
  156.0 3.1 copy-start.5
  162.8 3.1 copy-start.5
  169.7 1.3 copy-start.1
  171.0 160.7 %all-gather.8.cloned.1.call-start = ((), (), s32[]{:S(2)}) async-start(), calls=%async_computation.5 | async-start | bytes 1179648 | tf_op jit(solution)/shard_map/all_gather | solution.py:37
  288.4 162.1 %reduce-scatter.5.cloned.1.call-start = ((), (), s32[]{:S(2)}) async-start(), calls=%async_computation.6 | async-start | bytes 2228224 | tf_op jit(solution)/shard_map/reduce_scatter | solution.py:38
  331.8 118.7 %copy-start.2 = (f32[256,128]{1,0:T(8,128)S(1)}, f32[256,128]{1,0:T(8,128)}, u32[]{:S(2)}) copy-start(f32[256,128]{1,0:T(8,128)} %reduce-scatter.3.cloned.1.call-done) | copy-start | bytes 393220
  331.8 3.1 copy-start.6
  338.7 3.1 copy-start.6
  345.6 3.1 copy-start.6
  352.4 3.1 copy-start.6
  359.3 3.1 copy-start.6
  366.1 3.1 copy-start.6
  373.0 3.1 copy-start.6
  379.8 3.1 copy-start.6
  386.7 1.4 copy-start
  505.7 0.8 copy-start.4
Sparse Core Ops, SparseCore 0:
  10.9 48.0 all-gather.5
  61.3 53.3 all-gather.3
  171.1 60.3 reduce-scatter.2
  288.5 43.0 all-gather.7
  388.2 62.3 reduce-scatter.4
